TPU v7x, 128 devices: a whole 4x4x4 slice. The times are simulated.
128 devices in a mesh: expert: 32 (over z, y, core), helper: 4 (over x).
Axes of the slice: x: 4, y: 4, z: 4, core: 2. Of those that a mesh axis runs over, the one named last changes fastest.
Arguments:
- tokens: bfloat16 [131072, 768], P(('expert', 'helper')), may hold values from -6 to 6
- gate: float32 [131072], P(('expert', 'helper')), may hold values from 0.2 to 1
- expert_ids: int32 [131072, 1], P(('expert', 'helper')), may hold values from 0 to 127; in each aligned block of 1024 rows (0 to 1023, 1024 to 2047, ...) at most 12 rows name the same one
- backup_ids: int32 [131072, 1], P(('expert', 'helper')), may hold values from 0 to 127; in each aligned block of 1024 rows (0 to 1023, 1024 to 2047, ...) at most 12 rows name the same one
- capacity: int32 [128], replicated, may hold values from 2 to 12
- w_in: bfloat16 [128, 768, 3072], P('expert', None, 'helper'), may hold values from -0.21875 to 0.21875
- w_out: bfloat16 [128, 3072, 768], P('expert', 'helper'), may hold values from -0.109375 to 0.109375
Outputs:
- mixed: bfloat16 [131072, 768], P(('expert', 'helper'))
Inputs may be any that keep to these rules, and one draw needn't show every extreme that they name: `expert_ids`: in the rows of one device no expert is the first expert of more than 12 rows; some expert reaches 12. `backup_ids`: in the rows of one device no expert is the backup of more than 12 rows; some expert reaches 12.
All inputs are finite; a program needn't handle non-finite values.
Results may differ from a plain program's by a relative error of at most 0.0095.
Values may be sent and summed in bfloat16 or wider, within the bound.
No kernel may reach another device: no remote copies, remote signals or barrier semaphores. Data moves between devices by JAX's collectives and lax.ppermute only.
A program may use at most 192 MiB of HBM per device.

v0:
```python
import jax
import jax.numpy as jnp
from jax import lax
from jax.sharding import Mesh
from jax.sharding import PartitionSpec as P

EXPERT = ("expert_0", "expert_1", "expert_2")
EXPERT_HELPER = ("expert_0", "expert_1", "expert_2", "helper")


def split_up(array, dim, size):
    dims = array.shape
    parts = array.reshape(*dims[:dim], size, dims[dim] // size, *dims[dim + 1 :])
    return jnp.moveaxis(parts, dim, 0)


def laid_out(parts, dim):
    parts = jnp.moveaxis(parts, 0, dim)
    dims = parts.shape
    return parts.reshape(*dims[:dim], dims[dim] * dims[dim + 1], *dims[dim + 2 :])


def exchange_in_order(parts, axes, order):
    dims = [lax.axis_size(a) for a in axes]
    parts = parts.reshape(*dims, *parts.shape[1:])
    for k in order:
        parts = lax.all_to_all(parts, axes[k], split_axis=k, concat_axis=k, tiled=True)
    return parts.reshape(-1, *parts.shape[len(axes) :])


def core_and_chips(array, groups, order, split_dim, concat_dim):
    size = lax.axis_size(groups[0]) * lax.axis_size(groups[1])
    parts = split_up(array, split_dim, size)
    return laid_out(exchange_in_order(parts, groups, order), concat_dim)


def assign(first, backup, capacity, count, slot):
    columns = jnp.arange(count, dtype=jnp.int32)
    onehot = (first[:, None] == columns[None, :]).astype(jnp.int32)
    rank = jnp.sum((jnp.cumsum(onehot, axis=0) - onehot) * onehot, axis=1)
    limit = jnp.sum(onehot * capacity[None, :], axis=1)
    kept = rank < limit
    spill = (backup[:, None] == columns[None, :]).astype(jnp.int32) * (1 - kept.astype(jnp.int32))[
        :, None
    ]
    spill_rank = jnp.sum((jnp.cumsum(spill, axis=0) - spill) * spill, axis=1)
    final = jnp.where(kept, first, backup)
    slots = jnp.where(kept, rank, slot + spill_rank)
    return (slots, final)


def quarter_term(rows, weight_in, weight_out):
    hidden = jax.nn.relu(jnp.dot(rows, weight_in, preferred_element_type=jnp.float32)).astype(
        jnp.bfloat16
    )
    return jnp.dot(hidden, weight_out, preferred_element_type=jnp.float32)


def on_device(tokens, gate, expert_ids, backup_ids, capacity, w_in, w_out):
    held = w_in.shape[0]
    experts = held * lax.axis_size(EXPERT)
    helpers = lax.axis_size("helper")
    slot = max(6, 3 * tokens.shape[0] // (2 * experts))
    slots, final = assign(expert_ids[:, 0], backup_ids[:, 0], capacity, experts, slot)
    buffer = (
        jnp.zeros((2 * slot, experts, tokens.shape[1]), jnp.bfloat16).at[slots, final].set(tokens)
    )
    arrived = core_and_chips(buffer, (("expert_0", "expert_1"), "expert_2"), (1, 0), 1, 0)
    whole_in, whole_out = (
        lax.all_gather(w_in, "helper", axis=2, tiled=True),
        lax.all_gather(w_out, "helper", axis=1, tiled=True),
    )
    width = whole_in.shape[2] // helpers
    outputs = []
    for expert in range(held):
        total = jnp.zeros((arrived.shape[0], arrived.shape[2]), jnp.float32)
        for quarter in range(helpers):
            part = quarter_term(
                arrived[:, expert],
                whole_in[expert, :, quarter * width : (quarter + 1) * width],
                whole_out[expert, quarter * width : (quarter + 1) * width, :],
            )
            total = total + part.astype(jnp.bfloat16).astype(jnp.float32)
        outputs.append(total.astype(jnp.bfloat16))
    result = jnp.stack(outputs, axis=1)
    returned = core_and_chips(result, (("expert_0", "expert_1"), "expert_2"), (1, 0), 0, 1)
    picked = returned[slots, final]
    return (gate[:, None] * picked.astype(jnp.float32)).astype(jnp.bfloat16)


def solution(mesh):
    torus = Mesh(
        mesh.devices.reshape(4, 4, 2, mesh.shape["helper"]),
        ("expert_0", "expert_1", "expert_2", "helper"),
    )
    in_specs = (
        P(EXPERT_HELPER, None),
        P(EXPERT_HELPER),
        P(EXPERT_HELPER, None),
        P(EXPERT_HELPER, None),
        P(),
        P(EXPERT, None, "helper"),
        P(EXPERT, "helper", None),
    )
    out_specs = P(EXPERT_HELPER, None)
    return jax.shard_map(
        on_device, mesh=torus, in_specs=in_specs, out_specs=out_specs, check_vma=False
    )
```

profile of v0, /device:TPU:0, one launch (start us, length us, event | category | flops | bytes accessed | tf_op | source)
XLA Modules:
  0.0 538.9 jit_solution(8515442696640882063)
XLA Ops:
  6.5 0.7 all-gather.3.cloned.1.call-update
  7.3 0.7 all-gather.5.cloned.1.call-update
  8.0 0.1 copy.32
  8.2 0.1 copy.30
  8.3 0.2 fusion.7
  8.6 0.1 copy.31
  8.7 0.5 select_reduce_fusion
  9.2 0.1 copy.33
  9.3 0.3 fusion.5
  9.7 0.1 copy.34
  9.9 0.5 fusion.2
  10.4 0.1 multiply_reduce_fusion
  10.5 0.1 and_reduce_fusion
  10.6 9.2 %scatter_custom_fusion = bf16[3072,768]{1,0:T(8,128)(2,1)} fusion(s32[1024]{0:T(1024)S(1)} %broadcast_select_fusion, bf16[1024,768]{1,0:T(8,128)(2,1)} %param.7, bf16[]{:T(256)} %constant.31.clone.1), kind=kCustom, calls=%fused_computation.4 | custom fusion | bytes 4719104
  19.9 9.3 %reshape.114 = bf16[24,32,4,768]{3,2,1,0:T(4,128)(2,1)} reshape(bf16[3072,768]{1,0:T(8,128)(2,1)} %scatter_custom_fusion) | data formatting | bytes 9437184 | tf_op jit(solution)/shard_map/reshape | solution.py:13
  29.2 6.7 %copy.35 = bf16[24,32,4,768]{3,0,2,1:T(8,128)(2,1)S(1)} copy(bf16[24,32,4,768]{3,2,1,0:T(4,128)(2,1)} %reshape.114) | data formatting | bytes 9437184 | tf_op jit(solution)/shard_map/reshape | solution.py:13
  35.8 0.3 copy.36
  36.2 7.5 %all_to_all.20 = bf16[16,2,24,4,768]{4,2,0,3,1:T(8,128)(2,1)S(1)} all-to-all(bf16[16,2,24,4,768]{4,2,0,3,1:T(8,128)(2,1)S(1)} %copy.36), channel_id=1, replica_groups=mesh['expert_0'=4,'expert_1'=4,'expert_2'=2,'helper'=4] {'expert_2'}, dimensions={1} | all-to-all | bytes 9437184 | tf_op jit(solution)/shard_map/all_to_all | solution.py:27
  43.7 0.5 copy.37
  44.2 64.8 %all_to_all.21 = bf16[16,2,24,4,768]{4,2,1,3,0:T(8,128)(2,1)S(1)} all-to-all(bf16[16,2,24,4,768]{4,2,1,3,0:T(8,128)(2,1)S(1)} %copy.37), channel_id=1, replica_groups=mesh['expert_0'=4,'expert_1'=4,'expert_2'=2,'helper'=4] {'expert_0','exp..., dimensions={0} | all-to-all | bytes 9437184 | tf_op jit(solution)/shard_map/all_to_all | solution.py:27
  109.0 2.5 copy.38
  111.5 72.4 %all-gather.3.cloned.1.call-done = bf16[4,768,3072]{2,1,0:T(8,128)(2,1)} async-done(((bf16[4,768,768]{2,1,0:T(8,128)(2,1)}), bf16[4,768,3072]{2,1,0:T(8,128)(2,1)}) %all-gather.3.cloned.1.call-update) | async-done | bytes 18874384 | tf_op jit(solution)/shard_map/all_gather | solution.py:70
  183.9 173.4 %all-gather.5.cloned.1.call-done = bf16[4,3072,768]{2,1,0:T(8,128)(2,1)} async-done(((bf16[4,768,768]{2,1,0:T(8,128)(2,1)}), bf16[4,3072,768]{2,1,0:T(8,128)(2,1)}) %all-gather.5.cloned.1.call-update) | async-done | bytes 18874384 | tf_op jit(solution)/shard_map/all_gather | solution.py:71
  357.3 4.1 convolution_convert_fusion.2
  361.4 5.1 convolution_convert_fusion.1
  366.5 5.1 convolution_convert_fusion
  371.7 4.1 convolution_convert_fusion.6
  375.8 5.1 convolution_convert_fusion.5
  380.9 5.2 convolution_convert_fusion.4
  386.1 5.1 convolution_convert_fusion.10
  391.2 5.4 convolution_convert_fusion.9
  396.5 5.2 convolution_convert_fusion.8
  401.7 5.1 convolution_convert_fusion.14
  406.8 5.1 convolution_convert_fusion.13
  411.9 5.1 convolution_convert_fusion.12
  417.1 4.9 add_convert_fusion
  422.0 4.9 add_convert_fusion.1
  426.9 5.2 add_convert_fusion.2
  432.1 6.5 %add_convert_fusion.3 = bf16[768,768]{1,0:T(8,128)(2,1)} fusion(bf16[768,768]{1,0:T(8,128)(2,1)} %convolution_convert_fusion.12, bf16[768,768]{1,0:T(8,128)(2,1)} %convolution_convert_fusion.13, bf16[768,768]{1,0:T(8,128)(2,1)} %convolution_convert_fusion.14, bf16[4,3072,768]{2,1,0:T(8,128)(2,1)} %all-gather.5.cloned.1.call-done, ...), kind=kOutput, calls=%fused_computation.21 | convolution fusion | flops 1818427392 | bytes 8257536 | tf_op jit(solution)/shard_map/dot_general | solution.py:56
  438.7 1.7 pad_maximum_fusion
  440.3 0.3 copy.46
  440.7 7.5 %all_to_all.22 = bf16[16,2,24,4,768]{4,2,0,3,1:T(8,128)(2,1)S(1)} all-to-all(bf16[16,2,24,4,768]{4,2,0,3,1:T(8,128)(2,1)S(1)} %copy.46), channel_id=1, replica_groups=mesh['expert_0'=4,'expert_1'=4,'expert_2'=2,'helper'=4] {'expert_2'}, dimensions={1} | all-to-all | bytes 9437184 | tf_op jit(solution)/shard_map/all_to_all | solution.py:27
  448.2 0.5 copy.43
  448.7 63.6 %all_to_all.23 = bf16[16,2,24,4,768]{4,2,1,3,0:T(8,128)(2,1)S(1)} all-to-all(bf16[16,2,24,4,768]{4,2,1,3,0:T(8,128)(2,1)S(1)} %copy.43), channel_id=1, replica_groups=mesh['expert_0'=4,'expert_1'=4,'expert_2'=2,'helper'=4] {'expert_0','exp..., dimensions={0} | all-to-all | bytes 9437184 | tf_op jit(solution)/shard_map/all_to_all | solution.py:27
  512.3 0.6 copy.44
  512.8 3.2 copy.47
  516.0 14.3 %gather_fusion = bf16[1024,768]{1,0:T(8,128)(2,1)S(1)} fusion(bf16[24,128,768]{2,1,0:T(8,128)(2,1)} %copy.47, s32[1024]{0:T(1024)S(1)} %bitcast.231), kind=kCustom, calls=%fused_computation | custom fusion | bytes 3153920 | tf_op jit(solution)/shard_map/gather | solution.py:87
  530.4 1.5 multiply_convert_fusion
  (26 shorter events, 0.3 us)
Async XLA Ops:
  6.5 177.4 %all-gather.3.cloned.1.call-start = ((), (), s32[]{:S(2)}) async-start(), calls=%async_computation.4 | async-start | bytes 23592960 | tf_op jit(solution)/shard_map/all_gather | solution.py:70
  7.3 0.8 copy-start.1
  7.3 0.9 copy-start
  7.3 350.0 %all-gather.5.cloned.1.call-start = ((), (), s32[]{:S(2)}) async-start(), calls=%async_computation.5 | async-start | bytes 23592960 | tf_op jit(solution)/shard_map/all_gather | solution.py:71
  8.0 0.7 copy-start.3
  8.5 1.9 copy-start.5
  8.6 1.9 copy-start.4
  516.0 14.3 %copy-start.2 = (f32[1024]{0:T(1024)S(1)}, f32[1024]{0:T(1024)}, u32[]{:S(2)}) copy-start(f32[1024]{0:T(1024)} %param.8) | copy-start | bytes 12292
Sparse Core Ops, SparseCore 0:
  9.0 174.8 all-gather.2
  185.6 171.6 all-gather.4
where the time goes:
time: 545 us; the launch traced here: 539 us
  waiting for transfers between devices  247 us (45%)
  blocking collectives  143 us (26%)
  matrix products  81.3 us (15%)
  local copies, waits for them, and re-layouts  48 us (9%)
  between operations  13.9 us (3%)
    all_gather x1, waiting for transfers between devices, on_device(): lax.all_gather(w_out, 'helper', axis=1, tiled=True)  173 us
    all_to_all x4, blocking collectives, exchange_in_order(): lax.all_to_all(parts, axes[k], split_axis=k, concat_axis=k, tiled=True)  143 us
    dot_general x16, matrix products, quarter_term(): return jnp.dot(hidden, weight_out, preferred_element_type=jnp.float32)  81.3 us
    all_gather x1, waiting for transfers between devices, on_device(): lax.all_gather(w_in, 'helper', axis=2, tiled=True)  72.4 us
    reshape x2, local copies, waits for them, and re-layouts, split_up(): parts = array.reshape(*dims[:dim], size, dims[dim] // size, *dims[dim + 1:])  16 us
    gather x1, local copies, waits for them, and re-layouts, on_device(): picked = returned[slots, final]  14.3 us
  transfers between devices with their start and end apart: 2, of which 2 were waited for; matrix products, arithmetic and copies ran while one was open for 6% of the time, Pallas kernels for 0%

commit v1 on v0

--- a/solution.py
+++ b/solution.py
@@ -6,6 +6,11 @@
 
 EXPERT = ("expert_0", "expert_1", "expert_2")
 EXPERT_HELPER = ("expert_0", "expert_1", "expert_2", "helper")
+
+
+def all_by_exchange(x, axis, dim):
+    outgoing = jnp.stack([x] * lax.axis_size(axis))
+    return jnp.concatenate(lax.all_to_all(outgoing, axis, 0, 0), axis=dim)
 
 
 def split_up(array, dim, size):
@@ -67,7 +72,7 @@
     )
     arrived = core_and_chips(buffer, (("expert_0", "expert_1"), "expert_2"), (1, 0), 1, 0)
     whole_in, whole_out = (
-        lax.all_gather(w_in, "helper", axis=2, tiled=True),
+        all_by_exchange(w_in, "helper", 2),
         lax.all_gather(w_out, "helper", axis=1, tiled=True),
     )
     width = whole_in.shape[2] // helpers

time: 545 us -> 591 us (1.084)
  blocking collectives: 143 us -> 78.6 us
  waiting for transfers between devices: 247 us -> 305 us
  local copies, waits for them, and re-layouts: 48 us -> 84.8 us
  starting transfers between devices: 0.04 us -> 15.8 us
    all_to_all x0 -> x2, waiting for transfers between devices: none -> 304 us  [the longest x1 240 us: all_by_exchange(): return jnp.concatenate(lax.all_to_all(outgoing, axis, 0, 0), axis=dim)]
    all_gather x1, waiting for transfers between devices: 173 us -> 0.02 us  [on_device(): lax.all_gather(w_out, 'helper', axis=1, tiled=True)]
    all_gather x1 -> x0, waiting for transfers between devices: 72.4 us -> none  [on_device(): lax.all_gather(w_in, 'helper', axis=2, tiled=True)]
    all_to_all x4 -> x3, blocking collectives: 143 us -> 78.6 us  [exchange_in_order(): lax.all_to_all(parts, axes[k], split_axis=k, concat_axis=k, tiled=True)]
    all_to_all x0 -> x1, local copies, waits for them, and re-layouts: none -> 17.1 us  [all_by_exchange(): return jnp.concatenate(lax.all_to_all(outgoing, axis, 0, 0), axis=dim)]
    all_to_all x0 -> x2, starting transfers between devices: none -> 15.8 us  [the longest x1 8.31 us: exchange_in_order(): lax.all_to_all(parts, axes[k], split_axis=k, concat_axis=k, tiled=True)]
    another operation x6 -> x7, local copies, waits for them, and re-layouts: 0.22 us -> 8.59 us  [the longest x1 8.37 us: all_by_exchange(): outgoing = jnp.stack([x] * lax.axis_size(axis))]
    unnamed x13 -> x14, local copies, waits for them, and re-layouts: 9.27 us -> 16.1 us
  transfers between devices with their start and end apart: 2 -> 3, of which waited for: 2 -> 2; matrix products, arithmetic and copies ran while one was open for 6% -> 12% of each run, Pallas kernels for 0% -> 0%
where the time goes in v1:
time: 591 us; the launch traced here: 585 us
  waiting for transfers between devices  305 us (52%)
  local copies, waits for them, and re-layouts  84.8 us (14%)
  matrix products  81.7 us (14%)
  blocking collectives  78.6 us (13%)
  starting transfers between devices  15.8 us (3%)
  between operations  14 us (2%)
    all_to_all x1, waiting for transfers between devices, all_by_exchange(): return jnp.concatenate(lax.all_to_all(outgoing, axis, 0, 0), axis=dim)  240 us
    dot_general x16, matrix products, quarter_term(): return jnp.dot(hidden, weight_out, preferred_element_type=jnp.float32)  81.7 us
    all_to_all x3, blocking collectives, exchange_in_order(): lax.all_to_all(parts, axes[k], split_axis=k, concat_axis=k, tiled=True)  78.6 us
    all_to_all x1, waiting for transfers between devices, exchange_in_order(): lax.all_to_all(parts, axes[k], split_axis=k, concat_axis=k, tiled=True)  64.5 us
    all_to_all x1, local copies, waits for them, and re-layouts, all_by_exchange(): return jnp.concatenate(lax.all_to_all(outgoing, axis, 0, 0), axis=dim)  17.1 us
    unnamed x14, local copies, waits for them, and re-layouts  16.1 us
    reshape x2, local copies, waits for them, and re-layouts, split_up(): parts = array.reshape(*dims[:dim], size, dims[dim] // size, *dims[dim + 1:])  16 us
    gather x1, local copies, waits for them, and re-layouts, on_device(): picked = returned[slots, final]  14.3 us
  transfers between devices with their start and end apart: 3, of which 2 were waited for; matrix products, arithmetic and copies ran while one was open for 12% of the time, Pallas kernels for 0%

profile of v1, /device:TPU:0, one launch (start us, length us, event | category | flops | bytes accessed | tf_op | source)
XLA Modules:
  0.0 584.6 jit_solution(16576069486488683188)
XLA Ops:
  6.5 0.7 all-gather.2.cloned.1.call-update
  7.3 0.1 copy.33
  7.4 0.2 fusion.7
  7.7 0.1 copy.34
  7.9 0.5 select_reduce_fusion
  8.4 0.1 copy.36
  8.6 0.3 fusion.5
  9.1 0.1 copy.37
  9.2 0.5 fusion.2
  9.9 9.2 %scatter_custom_fusion = bf16[3072,768]{1,0:T(8,128)(2,1)} fusion(s32[1024]{0:T(1024)S(1)} %broadcast_select_fusion, bf16[1024,768]{1,0:T(8,128)(2,1)} %param.7, bf16[]{:T(256)} %constant.31.clone.1), kind=kCustom, calls=%fused_computation.4 | custom fusion | bytes 4719104
  19.2 9.4 %reshape.122 = bf16[24,32,4,768]{3,2,1,0:T(4,128)(2,1)} reshape(bf16[3072,768]{1,0:T(8,128)(2,1)} %scatter_custom_fusion) | data formatting | bytes 9437184 | tf_op jit(solution)/shard_map/reshape | solution.py:18
  28.6 6.7 %copy.38 = bf16[24,32,4,768]{3,0,2,1:T(8,128)(2,1)S(1)} copy(bf16[24,32,4,768]{3,2,1,0:T(4,128)(2,1)} %reshape.122) | data formatting | bytes 9437184 | tf_op jit(solution)/shard_map/reshape | solution.py:18
  35.2 0.3 copy.39
  35.6 7.5 %all_to_all.25 = bf16[16,2,24,4,768]{4,2,0,3,1:T(8,128)(2,1)S(1)} all-to-all(bf16[16,2,24,4,768]{4,2,0,3,1:T(8,128)(2,1)S(1)} %copy.39), channel_id=1, replica_groups=mesh['expert_0'=4,'expert_1'=4,'expert_2'=2,'helper'=4] {'expert_2'}, dimensions={1} | all-to-all | bytes 9437184 | tf_op jit(solution)/shard_map/all_to_all | solution.py:32
  43.1 2.7 copy.40
  45.7 8.3 %all-to-all-start.1 = ((bf16[16,2,24,4,768]{4,2,1,3,0:T(8,128)(2,1)}), bf16[16,2,24,4,768]{4,2,1,3,0:T(8,128)(2,1)}, u32[]{:S(2)}, u32[]{:S(2)}) async-start(bf16[16,2,24,4,768]{4,2,1,3,0:T(8,128)(2,1)} %copy.40), calls=%async_computation.1 | async-start | bytes 9437184 | tf_op jit(solution)/shard_map/all_to_all | solution.py:32
  54.1 6.7 %copy.42 = bf16[4,768,768]{1,2,0:T(8,128)(2,1)} copy(bf16[4,768,768]{2,1,0:T(8,128)(2,1)} %param.12) | data formatting | bytes 9437184 | tf_op args[5]
  60.8 64.5 %all-to-all-done.1 = bf16[16,2,24,4,768]{4,2,1,3,0:T(8,128)(2,1)} async-done(((bf16[16,2,24,4,768]{4,2,1,3,0:T(8,128)(2,1)}), bf16[16,2,24,4,768]{4,2,1,3,0:T(8,128)(2,1)}, u32[]{:S(2)}, u32[]{:S(2)}) %all-to-all-start.1) | async-done | bytes 4718624 | tf_op jit(solution)/shard_map/all_to_all | solution.py:32
  125.2 8.4 %stack.22 = bf16[4,4,768,768]{2,3,1,0:T(8,128)(2,1)} broadcast(bf16[4,768,768]{1,2,0:T(8,128)(2,1)} %copy.42), dimensions={1,2,3} | broadcast | bytes 23592960 | tf_op jit(solution)/shard_map/stack | solution.py:12
  133.6 7.5 %all-to-all-start.2 = ((bf16[4,4,768,768]{2,3,1,0:T(8,128)(2,1)}), bf16[4,4,768,768]{2,3,1,0:T(8,128)(2,1)}, u32[]{:S(2)}, u32[]{:S(2)}) async-start(bf16[4,4,768,768]{2,3,1,0:T(8,128)(2,1)} %stack.22), calls=%async_computation.2 | async-start | bytes 37748736 | tf_op jit(solution)/shard_map/all_to_all | solution.py:13
  141.1 4.9 copy.41
  146.0 239.5 %all-to-all-done.2 = bf16[4,4,768,768]{2,3,1,0:T(8,128)(2,1)} async-done(((bf16[4,4,768,768]{2,3,1,0:T(8,128)(2,1)}), bf16[4,4,768,768]{2,3,1,0:T(8,128)(2,1)}, u32[]{:S(2)}, u32[]{:S(2)}) %all-to-all-start.2) | async-done | bytes 18874400 | tf_op jit(solution)/shard_map/all_to_all | solution.py:13
  385.5 17.1 %copy.43 = bf16[4,4,768,768]{2,3,0,1:T(8,128)(2,1)} copy(bf16[4,4,768,768]{2,3,1,0:T(8,128)(2,1)} %all-to-all-done.2) | data formatting | bytes 37748736 | tf_op jit(solution)/shard_map/all_to_all | solution.py:13
  402.6 4.1 convolution_convert_fusion.14
  406.7 5.2 convolution_convert_fusion.13
  411.9 5.2 convolution_convert_fusion.12
  417.1 4.1 convolution_convert_fusion.10
  421.2 5.2 convolution_convert_fusion.9
  426.4 5.1 convolution_convert_fusion.8
  431.5 5.2 convolution_convert_fusion.6
  436.7 5.2 convolution_convert_fusion.5
  441.9 5.4 convolution_convert_fusion.4
  447.3 5.1 convolution_convert_fusion.2
  452.4 5.1 convolution_convert_fusion.1
  457.5 5.1 convolution_convert_fusion
  462.7 4.9 add_convert_fusion.3
  467.6 5.0 add_convert_fusion.2
  472.6 5.2 add_convert_fusion.1
  477.8 6.5 %add_convert_fusion = bf16[768,768]{1,0:T(8,128)(2,1)} fusion(bf16[768,768]{1,0:T(8,128)(2,1)} %convolution_convert_fusion, bf16[768,768]{1,0:T(8,128)(2,1)} %convolution_convert_fusion.1, bf16[768,768]{1,0:T(8,128)(2,1)} %convolution_convert_fusion.2, bf16[4,3072,768]{2,1,0:T(8,128)(2,1)} %all-gather.2.cloned.1.call-done, ...), kind=kOutput, calls=%fused_computation.6 | convolution fusion | flops 1818427392 | bytes 8257536 | tf_op jit(solution)/shard_map/dot_general | solution.py:61
  484.4 1.7 pad_maximum_fusion
  486.1 0.3 copy.51
  486.4 7.5 %all_to_all.26 = bf16[16,2,24,4,768]{4,2,0,3,1:T(8,128)(2,1)S(1)} all-to-all(bf16[16,2,24,4,768]{4,2,0,3,1:T(8,128)(2,1)S(1)} %copy.51), channel_id=1, replica_groups=mesh['expert_0'=4,'expert_1'=4,'expert_2'=2,'helper'=4] {'expert_2'}, dimensions={1} | all-to-all | bytes 9437184 | tf_op jit(solution)/shard_map/all_to_all | solution.py:32
  493.9 0.5 copy.48
  494.4 63.6 %all_to_all.27 = bf16[16,2,24,4,768]{4,2,1,3,0:T(8,128)(2,1)S(1)} all-to-all(bf16[16,2,24,4,768]{4,2,1,3,0:T(8,128)(2,1)S(1)} %copy.48), channel_id=1, replica_groups=mesh['expert_0'=4,'expert_1'=4,'expert_2'=2,'helper'=4] {'expert_0','exp..., dimensions={0} | all-to-all | bytes 9437184 | tf_op jit(solution)/shard_map/all_to_all | solution.py:32
  558.0 0.6 copy.49
  558.6 3.2 copy.52
  561.7 14.3 %gather_fusion = bf16[1024,768]{1,0:T(8,128)(2,1)S(1)} fusion(bf16[24,128,768]{2,1,0:T(8,128)(2,1)} %copy.52, s32[1024]{0:T(1024)S(1)} %bitcast.233), kind=kCustom, calls=%fused_computation | custom fusion | bytes 3153920 | tf_op jit(solution)/shard_map/gather | solution.py:92
  576.1 1.5 multiply_convert_fusion
  (29 shorter events, 0.6 us)
Async XLA Ops:
  6.5 0.7 copy-start
  6.5 396.1 %all-gather.2.cloned.1.call-start = ((), (), s32[]{:S(2)}) async-start(), calls=%async_computation.5 | async-start | bytes 23592960 | tf_op jit(solution)/shard_map/all_gather | solution.py:76
  7.3 0.7 copy-start.3
  7.3 1.3 copy-start.1
  7.7 2.0 copy-start.5
  7.7 2.1 copy-start.4
  45.7 79.5 %all-to-all-start.1 = ((bf16[16,2,24,4,768]{4,2,1,3,0:T(8,128)(2,1)}), bf16[16,2,24,4,768]{4,2,1,3,0:T(8,128)(2,1)}, u32[]{:S(2)}, u32[]{:S(2)}) async-start(bf16[16,2,24,4,768]{4,2,1,3,0:T(8,128)(2,1)} %copy.40), calls=%async_computation.1 | async-start | bytes 9437184 | tf_op jit(solution)/shard_map/all_to_all | solution.py:32
  133.6 251.9 %all-to-all-start.2 = ((bf16[4,4,768,768]{2,3,1,0:T(8,128)(2,1)}), bf16[4,4,768,768]{2,3,1,0:T(8,128)(2,1)}, u32[]{:S(2)}, u32[]{:S(2)}) async-start(bf16[4,4,768,768]{2,3,1,0:T(8,128)(2,1)} %stack.22), calls=%async_computation.2 | async-start | bytes 37748736 | tf_op jit(solution)/shard_map/all_to_all | solution.py:13
  561.7 14.3 %copy-start.2 = (f32[1024]{0:T(1024)S(1)}, f32[1024]{0:T(1024)}, u32[]{:S(2)}) copy-start(f32[1024]{0:T(1024)} %param.8) | copy-start | bytes 12292
Sparse Core Ops, SparseCore 0:
  9.0 212.6 all-gather.1
